TPU v7x, 256 devices: a whole 4x4x8 slice. The times are simulated.
256 devices in a mesh: dp: 32 (over y, z), vocab: 8 (over x, core).
Axes of the slice: x: 4, y: 4, z: 8, core: 2. Of those that a mesh axis runs over, the one named last changes fastest.
Arguments:
- hidden: bfloat16 [24576, 2048], P('dp', 'vocab')
- gain: bfloat16 [2048], replicated, may hold values from 0.5 to 1.5
- head: bfloat16 [2048, 32000], P('dp', 'vocab')
- target_ids: int32 [24576], P('dp'), may hold values from 0 to 31999
- seq_lens: int32 [64], replicated, may hold values from 64 to 704, as said below
- seq_owner: int32 [64], replicated, may hold values from 0 to 31, as said below
Outputs:
- logprob: float32 [24576], P('dp')
- entropy: float32 [24576], P('dp')
Inputs may be any that keep to these rules, and one draw needn't show every extreme that they name: `seq_lens`: the lengths of the sequences owned by one dp index sum to at most 768; in every draw the sequences of some dp index sum to exactly 768. `seq_owner`: every dp index owns exactly 2 sequences.
All inputs are finite; a program needn't handle non-finite values.
Results may differ from a plain program's by a relative error of at most 0.0075.
Values may be sent and summed in bfloat16 or wider, within the bound.
A program may use at most 64 MiB of HBM per device.

v0:
```python
import jax
import jax.numpy as jnp
from jax import lax
from jax.sharding import PartitionSpec as P

EPS = 1e-05


def chunk_bounds(breadth, parts):
    step = -(-breadth // parts)
    step = -(-step // 128) * 128
    bounds = []
    start = 0
    while start < breadth:
        stop = min(start + step, breadth)
        bounds.append((start, stop))
        start = stop
    return bounds


def chunk_stats(normed, columns, local_id, start):
    logits = jnp.dot(normed, columns, preferred_element_type=jnp.float32)
    top = jnp.max(logits, axis=1)
    expo = jnp.exp(logits - top[:, None])
    total = jnp.sum(expo, axis=1)
    weighted = jnp.sum(expo * logits, axis=1)
    ids = start + lax.broadcasted_iota(jnp.int32, logits.shape, 1)
    picked = jnp.sum(jnp.where(ids == local_id[:, None], logits, 0.0), axis=1)
    return (top, total, weighted, picked)


def local(hidden, gain, head, target_ids, seq_lens, seq_owner):
    groups = lax.axis_size("dp")
    position = lax.axis_index("dp")
    slice_index = lax.axis_index("vocab")
    slots = hidden.shape[0]
    breadth = head.shape[1]
    owners = jnp.arange(groups, dtype=jnp.int32)
    loads = jnp.sum(jnp.where(seq_owner[:, None] == owners[None, :], seq_lens[:, None], 0), axis=0)
    own_live = jnp.arange(slots, dtype=jnp.int32) < loads[position]
    features = lax.all_gather(hidden, "vocab", axis=1, tiled=True)
    wide = features.astype(jnp.float32)
    normed = (
        wide
        * lax.rsqrt(jnp.mean(wide * wide, axis=1, keepdims=True) + EPS)
        * gain.astype(jnp.float32)
    ).astype(jnp.bfloat16)
    local_id = target_ids - slice_index * breadth
    parts = []
    for start, stop in chunk_bounds(breadth, 4):
        columns = lax.all_gather(head[:, start:stop], "dp", axis=0, tiled=True)
        parts.append(chunk_stats(normed, columns, local_id, start))
    tops = jnp.stack([p[0] for p in parts])
    top_local = jnp.max(tops, axis=0)
    scale = jnp.exp(tops - top_local[None, :])
    total_local = jnp.sum(jnp.stack([p[1] for p in parts]) * scale, axis=0)
    weighted_local = jnp.sum(jnp.stack([p[2] for p in parts]) * scale, axis=0)
    picked_local = jnp.sum(jnp.stack([p[3] for p in parts]), axis=0)
    top = lax.pmax(top_local, "vocab")
    factor = jnp.exp(top_local - top)
    total, weighted, picked = lax.psum(
        (total_local * factor, weighted_local * factor, picked_local), "vocab"
    )
    lse = top + jnp.log(total)
    logprob = picked - lse
    entropy = lse - weighted / total
    return (jnp.where(own_live, logprob, 0.0), jnp.where(own_live, entropy, 0.0))


def solution(mesh):
    return jax.shard_map(
        local,
        mesh=mesh,
        in_specs=(P("dp", "vocab"), P(), P("dp", "vocab"), P("dp"), P(), P()),
        out_specs=(P("dp"), P("dp")),
        check_vma=False,
    )
```

profile of v0, /device:TPU:32, one launch (start us, length us, event | category | flops | bytes accessed | tf_op | source)
XLA Modules:
  0.0 432.0 jit_solution(7421292452426967437)
XLA Ops:
  7.2 0.0 all-gather.6.cloned.1.call-start
  7.2 0.7 all-gather.6.cloned.1.call-update
  7.9 0.0 all-gather.14.cloned.1.call-start
  7.9 1.6 slice.15
  9.5 0.0 all-gather.14.cloned.1.call-update
  9.5 0.0 all-gather.8.cloned.1.call-start
  9.6 1.8 fusion.20
  11.4 0.0 all-gather.8.cloned.1.call-update
  11.4 0.0 all-gather.10.cloned.1.call-start
  11.5 0.5 all-gather.10.cloned.1.call-update
  12.0 0.0 all-gather.12.cloned.1.call-start
  12.0 0.5 all-gather.12.cloned.1.call-update
  12.6 0.7 convert_element_type.10
  13.3 0.8 select_reduce_fusion.4
  14.1 0.7 dynamic_slice.3
  14.7 0.7 broadcast_subtract_fusion
  15.4 31.2 %all-gather.6.cloned.1.call-done = bf16[768,2048]{1,0:T(8,128)(2,1)} async-done(((bf16[768,256]{1,0:T(8,128)(2,1)}), bf16[768,2048]{1,0:T(8,128)(2,1)}) %all-gather.6.cloned.1.call-update) | async-done | bytes 3145744 | tf_op jit(solution)/shard_map/all_gather | solution.py:41
  46.6 0.0 copy-start.1
  46.6 2.7 fusion
  49.4 82.9 %all-gather.14.cloned.1.call-done = bf16[2048,928]{1,0:T(8,128)(2,1)} async-done(((bf16[64,928]{1,0:T(8,128)(2,1)}), bf16[2048,928]{1,0:T(8,128)(2,1)}) %all-gather.14.cloned.1.call-update) | async-done | bytes 3801104 | tf_op jit(solution)/shard_map/all_gather | solution.py:51
  132.3 0.0 copy-done.1
  132.3 5.9 %fusion.21 = (f32[768]{0:T(1024)S(1)}, f32[768,928]{0,1:T(8,128)S(1)}) fusion(bf16[2048,928]{1,0:T(8,128)(2,1)} %all-gather.14.cloned.1.call-done, bf16[768,2048]{1,0:T(8,128)(2,1)S(1)} %copy-done.1, f32[2048]{0:T(1024)S(1)} %convert_element_type.10, f32[768]{0:T(1024)S(1)} %add_rsqrt_fusion), kind=kOutput, calls=%fused_computation.49 | convolution fusion | flops 2926238976 | bytes 9811968 | tf_op jit(solution)/shard_map/dot_general | solution.py:22
  138.2 0.9 multiply_reduce_fusion.3
  139.0 74.9 %all-gather.8.cloned.1.call-done = bf16[2048,1024]{1,0:T(8,128)(2,1)} async-done(((bf16[64,1024]{1,0:T(8,128)(2,1)}), bf16[2048,1024]{1,0:T(8,128)(2,1)}) %all-gather.8.cloned.1.call-update) | async-done | bytes 4194320 | tf_op jit(solution)/shard_map/all_gather | solution.py:51
  214.0 6.4 %fusion.24 = (f32[768]{0:T(1024)S(1)}, f32[768,1024]{1,0:T(8,128)S(1)}) fusion(bf16[2048,1024]{1,0:T(8,128)(2,1)} %all-gather.8.cloned.1.call-done, bf16[768,2048]{1,0:T(8,128)(2,1)} %all-gather.6.cloned.1.call-done, f32[2048]{0:T(1024)S(1)} %convert_element_type.10, f32[768]{0:T(1024)S(1)} %add_rsqrt_fusion), kind=kOutput, calls=%fused_computation.52 | convolution fusion | flops 3228302592 | bytes 10500096 | tf_op jit(solution)/shard_map/dot_general | solution.py:22
  220.4 75.1 %all-gather.10.cloned.1.call-done = bf16[2048,1024]{1,0:T(8,128)(2,1)} async-done(((bf16[64,1024]{1,0:T(8,128)(2,1)}), bf16[2048,1024]{1,0:T(8,128)(2,1)}) %all-gather.10.cloned.1.call-update) | async-done | bytes 4194320 | tf_op jit(solution)/shard_map/all_gather | solution.py:51
  295.5 8.4 %fusion.22 = (f32[768]{0:T(1024)S(1)}, f32[768,1024]{1,0:T(8,128)}) fusion(bf16[2048,1024]{1,0:T(8,128)(2,1)} %all-gather.10.cloned.1.call-done, bf16[768,2048]{1,0:T(8,128)(2,1)} %all-gather.6.cloned.1.call-done, f32[2048]{0:T(1024)S(1)} %convert_element_type.10, f32[768]{0:T(1024)S(1)} %add_rsqrt_fusion), kind=kOutput, calls=%fused_computation.50 | convolution fusion | flops 3228302592 | bytes 10500096 | tf_op jit(solution)/shard_map/dot_general | solution.py:22
  303.8 73.2 %all-gather.12.cloned.1.call-done = bf16[2048,1024]{1,0:T(8,128)(2,1)} async-done(((bf16[64,1024]{1,0:T(8,128)(2,1)}), bf16[2048,1024]{1,0:T(8,128)(2,1)}) %all-gather.12.cloned.1.call-update) | async-done | bytes 4194320 | tf_op jit(solution)/shard_map/all_gather | solution.py:51
  377.0 0.0 copy-start
  377.0 6.6 %fusion.23 = (f32[768]{0:T(1024)S(1)}, f32[768,1024]{1,0:T(8,128)S(1)}) fusion(bf16[2048,1024]{1,0:T(8,128)(2,1)} %all-gather.12.cloned.1.call-done, bf16[768,2048]{1,0:T(8,128)(2,1)} %all-gather.6.cloned.1.call-done, f32[2048]{0:T(1024)S(1)} %convert_element_type.10, f32[768]{0:T(1024)S(1)} %add_rsqrt_fusion), kind=kOutput, calls=%fused_computation.51 | convolution fusion | flops 3228302592 | bytes 10500096 | tf_op jit(solution)/shard_map/dot_general | solution.py:22
  383.6 0.0 copy-done
  383.6 4.4 %multiply_reduce_fusion.1 = (f32[768]{0:T(1024)S(1)}, f32[768]{0:T(1024)S(1)}, f32[768]{0:T(1024)S(1)}, f32[768]{0:T(1024)S(1)}, f32[768]{0:T(1024)S(1)}, /*inde...) fusion(f32[768,1024]{1,0:T(8,128)S(1)} %copy-done, f32[768]{0:T(1024)S(1)} %get-tuple-element.34, ...), kind=kLoop, calls=%fused_computation.6 | loop fusion | flops 16508160 | bytes 9485312 | tf_op jit(solution)/shard_map/reduce_sum | solution.py:26
  388.1 12.4 %pmax.7 = f32[768]{0:T(1024)S(1)} all-reduce(f32[768]{0:T(1024)S(1)} %maximum_maximum_fusion), channel_id=1, replica_groups=mesh['dp'=32,'vocab'=8] {'vocab'}, use_global_device_ids=true, to_apply=%region_11.12 | all-reduce | flops 768 | bytes 6144 | tf_op jit(solution)/shard_map/pmax | solution.py:59
  400.5 0.1 fusion.9
  400.6 23.6 %all-reduce = (f32[768]{0:T(1024)S(1)}, f32[768]{0:T(1024)S(1)}, f32[768]{0:T(1024)S(1)}) all-reduce(f32[768]{0:T(1024)S(1)} %add_add_fusion, f32[768]{0:T(1024)S(1)} %get-tuple-element.25, f32[768]{0:T(1024)S(1)} %get-tuple-element.24), channel_id=1, replica_groups=mesh['dp'=32,'vocab'=8] {'vocab'}, use_global_device_ids=true, to_apply=%region_6.7 | all-reduce | flops 2304 | bytes 18432 | tf_op jit(solution)/shard_map/psum | solution.py:61
  424.2 1.3 subtract_select_fusion
  (18 shorter events, 0.1 us)
Async XLA Ops:
  7.2 39.5 %all-gather.6.cloned.1.call-start = ((), (), s32[]{:S(2)}) async-start(), calls=%async_computation | async-start | bytes 3538944 | tf_op jit(solution)/shard_map/all_gather | solution.py:41
  7.9 124.4 %all-gather.14.cloned.1.call-start = ((), (), s32[]{:S(2)}) async-start(), calls=%async_computation.4 | async-start | bytes 4325376 | tf_op jit(solution)/shard_map/all_gather | solution.py:51
  9.5 204.4 %all-gather.8.cloned.1.call-start = ((), (), s32[]{:S(2)}) async-start(), calls=%async_computation.1 | async-start | bytes 4325376 | tf_op jit(solution)/shard_map/all_gather | solution.py:51
  11.4 284.1 %all-gather.10.cloned.1.call-start = ((), (), s32[]{:S(2)}) async-start(), calls=%async_computation.2 | async-start | bytes 4325376 | tf_op jit(solution)/shard_map/all_gather | solution.py:51
  12.0 365.0 %all-gather.12.cloned.1.call-start = ((), (), s32[]{:S(2)}) async-start(), calls=%async_computation.3 | async-start | bytes 4325376 | tf_op jit(solution)/shard_map/all_gather | solution.py:51
  46.6 85.6 %copy-start.1 = (bf16[768,2048]{1,0:T(8,128)(2,1)S(1)}, bf16[768,2048]{1,0:T(8,128)(2,1)}, u32[]{:S(2)}) copy-start(bf16[768,2048]{1,0:T(8,128)(2,1)} %all-gather.6.cloned.1.call-done) | copy-start | bytes 9437188
  377.0 6.6 %copy-start = (f32[768,1024]{1,0:T(8,128)S(1)}, f32[768,1024]{1,0:T(8,128)}, u32[]{:S(2)}) copy-start(f32[768,1024]{1,0:T(8,128)} %get-tuple-element.35) | copy-start | bytes 9437188
Sparse Core Ops, SparseCore 0:
  9.8 36.7 all-gather.5
  49.2 83.0 all-gather.13
  134.9 79.0 all-gather.7
  216.4 79.0 all-gather.9
  297.9 79.0 all-gather.11
where the time goes:
time: 432 us
  waiting for transfers between devices  339 us (78%)
  blocking collectives  36 us (8%)
  matrix products  27.2 us (6%)
  between operations  13.9 us (3%)
  other arithmetic  11.6 us (3%)
    all_gather x4, waiting for transfers between devices, local(): columns = lax.all_gather(head[:, start:stop], 'dp', axis=0, tiled=True)  306 us
    all_gather x1, waiting for transfers between devices, local(): features = lax.all_gather(hidden, 'vocab', axis=1, tiled=True)  31.2 us
    dot_general x4, matrix products, chunk_stats(): logits = jnp.dot(normed, columns, preferred_element_type=jnp.float32)  27.2 us
    psum x1, blocking collectives, local(): lax.psum((total_local * factor, weighted_local * factor, picked_local), '...  23.6 us
    pmax x1, blocking collectives, local(): top = lax.pmax(top_local, 'vocab')  12.4 us
  transfers between devices with their start and end apart: 5, of which 5 were waited for; matrix products, arithmetic and copies ran while one was open for 7% of the time, Pallas kernels for 0%

commit v1 on v0

--- a/solution.py
+++ b/solution.py
@@ -48,7 +48,9 @@
     local_id = target_ids - slice_index * breadth
     parts = []
     for start, stop in chunk_bounds(breadth, 4):
-        columns = lax.all_gather(head[:, start:stop], "dp", axis=0, tiled=True)
+        block = head[:, start:stop]
+        sent = jnp.stack([block] * lax.axis_size("dp"))
+        columns = jnp.concatenate(lax.all_to_all(sent, "dp", 0, 0), axis=0)
         parts.append(chunk_stats(normed, columns, local_id, start))
     tops = jnp.stack([p[0] for p in parts])
     top_local = jnp.max(tops, axis=0)

time: 432 us -> 485 us (1.12)
  blocking collectives: 36 us -> 141 us
  waiting for transfers between devices: 339 us -> 264 us
  starting transfers between devices: 0.2 us -> 23.5 us
  local copies, waits for them, and re-layouts: 4.11 us -> 9.7 us
    all_gather x4 -> x0, waiting for transfers between devices: 306 us -> none  [local(): columns = lax.all_gather(head[:, start:stop], 'dp', axis=0, tiled=True)]
    all_to_all x0 -> x3, waiting for transfers between devices: none -> 263 us  [local(): columns = jnp.concatenate(lax.all_to_all(sent, 'dp', 0, 0), axis=0)]
    all_to_all x0 -> x1, blocking collectives: none -> 102 us  [local(): columns = jnp.concatenate(lax.all_to_all(sent, 'dp', 0, 0), axis=0)]
    all_gather x1, waiting for transfers between devices: 31.2 us -> 0.02 us  [local(): features = lax.all_gather(hidden, 'vocab', axis=1, tiled=True)]
    all_to_all x0 -> x3, starting transfers between devices: none -> 23.5 us  [local(): columns = jnp.concatenate(lax.all_to_all(sent, 'dp', 0, 0), axis=0)]
    another operation x0 -> x4, local copies, waits for them, and re-layouts: none -> 7.98 us  [local(): sent = jnp.stack([block] * lax.axis_size('dp'))]
  transfers between devices with their start and end apart: 5 -> 4, of which waited for: 5 -> 3; matrix products, arithmetic and copies ran while one was open for 7% -> 5% of each run, Pallas kernels for 0% -> 0%
where the time goes in v1:
time: 485 us; the launch traced here: 484 us
  waiting for transfers between devices  264 us (54%)
  blocking collectives  141 us (29%)
  starting transfers between devices  23.5 us (5%)
  matrix products  23.2 us (5%)
  between operations  14.3 us (3%)
  local copies, waits for them, and re-layouts  9.7 us (2%)
  other arithmetic  9.24 us (2%)
    all_to_all x3, waiting for transfers between devices, local(): columns = jnp.concatenate(lax.all_to_all(sent, 'dp', 0, 0), axis=0)  263 us
    all_to_all x1, blocking collectives, local(): columns = jnp.concatenate(lax.all_to_all(sent, 'dp', 0, 0), axis=0)  102 us
    psum x1, blocking collectives, local(): lax.psum((total_local * factor, weighted_local * factor, picked_local), '...  23.6 us
    all_to_all x3, starting transfers between devices, local(): columns = jnp.concatenate(lax.all_to_all(sent, 'dp', 0, 0), axis=0)  23.5 us
    dot_general x4, matrix products, chunk_stats(): logits = jnp.dot(normed, columns, preferred_element_type=jnp.float32)  23.2 us
    pmax x1, blocking collectives, local(): top = lax.pmax(top_local, 'vocab')  14.7 us
  transfers between devices with their start and end apart: 4, of which 3 were waited for; matrix products, arithmetic and copies ran while one was open for 5% of the time, Pallas kernels for 0%

profile of v1, /device:TPU:32, one launch (start us, length us, event | category | flops | bytes accessed | tf_op | source)
XLA Modules:
  0.0 484.1 jit_solution(6710098460293923704)
XLA Ops:
  7.2 0.9 slice.15
  8.1 2.5 stack.41
  10.6 0.0 copy-start.3
  10.6 11.5 %all-to-all-start.3 = ((bf16[32,64,928]{2,1,0:T(8,128)(2,1)}), bf16[32,64,928]{2,1,0:T(8,128)(2,1)}, u32[]{:S(2)}, u32[]{:S(2)}) async-start(bf16[32,64,928]{2,1,0:T(8,128)(2,1)} %stack.41), calls=%async_computation.3 | async-start | bytes 8388608 | tf_op jit(solution)/shard_map/all_to_all | solution.py:53
  22.1 0.0 copy-done.3
  22.2 95.5 %all-to-all-done.3 = bf16[32,64,928]{2,1,0:T(8,128)(2,1)} async-done(((bf16[32,64,928]{2,1,0:T(8,128)(2,1)}), bf16[32,64,928]{2,1,0:T(8,128)(2,1)}, u32[]{:S(2)}, u32[]{:S(2)}) %all-to-all-start.3) | async-done | bytes 3801120 | tf_op jit(solution)/shard_map/all_to_all | solution.py:53
  117.7 0.5 stack.39
  118.2 102.4 %all_to_all.20 = bf16[32,64,1024]{2,1,0:T(8,128)(2,1)} all-to-all(bf16[32,64,1024]{2,1,0:T(8,128)(2,1)S(1)} %stack.39), channel_id=1, replica_groups=mesh['dp'=32,'vocab'=8] {'dp'}, dimensions={0} | all-to-all | bytes 8388608 | tf_op jit(solution)/shard_map/all_to_all | solution.py:53
  220.6 2.5 stack.38
  223.1 5.2 %all-to-all-start = ((bf16[32,64,1024]{2,1,0:T(8,128)(2,1)}), bf16[32,64,1024]{2,1,0:T(8,128)(2,1)}, u32[]{:S(2)}, u32[]{:S(2)}) async-start(bf16[32,64,1024]{2,1,0:T(8,128)(2,1)} %stack.38), calls=%async_computation | async-start | bytes 8388608 | tf_op jit(solution)/shard_map/all_to_all | solution.py:53
  228.3 0.0 all-gather.2.cloned.1.call-start
  228.4 0.7 all-gather.2.cloned.1.call-update
  229.1 94.3 %all-to-all-done = bf16[32,64,1024]{2,1,0:T(8,128)(2,1)} async-done(((bf16[32,64,1024]{2,1,0:T(8,128)(2,1)}), bf16[32,64,1024]{2,1,0:T(8,128)(2,1)}, u32[]{:S(2)}, u32[]{:S(2)}) %all-to-all-start) | async-done | bytes 4194336 | tf_op jit(solution)/shard_map/all_to_all | solution.py:53
  323.4 2.5 stack.40
  325.8 0.0 copy-start.4
  325.8 0.0 copy-start.6
  325.8 0.0 copy-start.7
  325.8 0.0 copy-start.5
  325.8 6.7 %all-to-all-start.2 = ((bf16[32,64,1024]{2,1,0:T(8,128)(2,1)}), bf16[32,64,1024]{2,1,0:T(8,128)(2,1)}, u32[]{:S(2)}, u32[]{:S(2)}) async-start(bf16[32,64,1024]{2,1,0:T(8,128)(2,1)} %stack.40), calls=%async_computation.2 | async-start | bytes 8388608 | tf_op jit(solution)/shard_map/all_to_all | solution.py:53
  332.5 0.0 copy-done.4
  332.5 0.0 copy-done.6
  332.5 0.0 copy-done.7
  332.6 0.1 select_reduce_fusion.4
  332.7 0.6 dynamic_slice.3
  333.3 0.0 copy-done.5
  333.3 0.0 all-gather.2.cloned.1.call-done
  333.3 0.0 copy-start.2
  333.3 2.7 fusion
  336.1 0.1 copy-done.2
  336.1 5.8 %fusion.21 = (f32[768]{0:T(1024)S(1)}, f32[768,928]{0,1:T(8,128)S(1)}) fusion(bf16[2048,928]{1,0:T(8,128)(2,1)} %bitcast.4, bf16[768,2048]{1,0:T(8,128)(2,1)S(1)} %copy-done.2, f32[2048]{0:T(1024)S(1)} %convert_element_type.10, f32[768]{0:T(1024)S(1)} %add_rsqrt_fusion), kind=kOutput, calls=%fused_computation.49 | convolution fusion | flops 2926238976 | bytes 9811968 | tf_op jit(solution)/shard_map/dot_general | solution.py:22
  342.0 0.9 multiply_reduce_fusion.3
  342.9 0.0 copy-start
  342.9 5.6 %fusion.24 = (f32[768]{0:T(1024)S(1)}, f32[768,1024]{1,0:T(8,128)S(1)}) fusion(bf16[2048,1024]{1,0:T(8,128)(2,1)} %bitcast.1, bf16[768,2048]{1,0:T(8,128)(2,1)S(1)} %copy-done.2, f32[2048]{0:T(1024)S(1)} %convert_element_type.10, f32[768]{0:T(1024)S(1)} %add_rsqrt_fusion), kind=kOutput, calls=%fused_computation.52 | convolution fusion | flops 3228302592 | bytes 10500096 | tf_op jit(solution)/shard_map/dot_general | solution.py:22
  348.5 0.0 copy-done
  348.6 5.2 %fusion.22 = (f32[768]{0:T(1024)S(1)}, f32[768,1024]{1,0:T(8,128)}) fusion(bf16[2048,1024]{1,0:T(8,128)(2,1)S(1)} %bitcast.9, bf16[768,2048]{1,0:T(8,128)(2,1)S(1)} %copy-done.2, f32[2048]{0:T(1024)S(1)} %convert_element_type.10, f32[768]{0:T(1024)S(1)} %add_rsqrt_fusion), kind=kOutput, calls=%fused_computation.50 | convolution fusion | flops 3228302592 | bytes 10500096 | tf_op jit(solution)/shard_map/dot_general | solution.py:22
  353.7 73.1 %all-to-all-done.2 = bf16[32,64,1024]{2,1,0:T(8,128)(2,1)} async-done(((bf16[32,64,1024]{2,1,0:T(8,128)(2,1)}), bf16[32,64,1024]{2,1,0:T(8,128)(2,1)}, u32[]{:S(2)}, u32[]{:S(2)}) %all-to-all-start.2) | async-done | bytes 4194336 | tf_op jit(solution)/shard_map/all_to_all | solution.py:53
  426.8 0.0 copy-start.1
  426.8 6.5 %fusion.23 = (f32[768]{0:T(1024)S(1)}, f32[768,1024]{1,0:T(8,128)S(1)}) fusion(bf16[2048,1024]{1,0:T(8,128)(2,1)} %bitcast.3, bf16[768,2048]{1,0:T(8,128)(2,1)} %all-gather.2.cloned.1.call-done, f32[2048]{0:T(1024)S(1)} %convert_element_type.10, f32[768]{0:T(1024)S(1)} %add_rsqrt_fusion), kind=kOutput, calls=%fused_computation.51 | convolution fusion | flops 3228302592 | bytes 10500096 | tf_op jit(solution)/shard_map/dot_general | solution.py:22
  433.4 0.0 copy-done.1
  433.4 4.3 multiply_reduce_fusion.1
  437.7 14.7 %pmax.7 = f32[768]{0:T(1024)S(1)} all-reduce(f32[768]{0:T(1024)S(1)} %maximum_maximum_fusion), channel_id=1, replica_groups=mesh['dp'=32,'vocab'=8] {'vocab'}, use_global_device_ids=true, to_apply=%region_11.12 | all-reduce | flops 768 | bytes 6144 | tf_op jit(solution)/shard_map/pmax | solution.py:61
  452.4 0.1 fusion.9
  452.5 23.6 %all-reduce = (f32[768]{0:T(1024)S(1)}, f32[768]{0:T(1024)S(1)}, f32[768]{0:T(1024)S(1)}) all-reduce(f32[768]{0:T(1024)S(1)} %add_add_fusion, f32[768]{0:T(1024)S(1)} %get-tuple-element.25, f32[768]{0:T(1024)S(1)} %get-tuple-element.24), channel_id=1, replica_groups=mesh['dp'=32,'vocab'=8] {'vocab'}, use_global_device_ids=true, to_apply=%region_6.7 | all-reduce | flops 2304 | bytes 18432 | tf_op jit(solution)/shard_map/psum | solution.py:63
  476.1 1.2 subtract_select_fusion
  (21 shorter events, 0.1 us)
Async XLA Ops:
  10.6 11.6 %copy-start.3 = (bf16[64,4000]{1,0:T(8,128)(2,1)S(1)}, bf16[64,4000]{1,0:T(8,128)(2,1)}, u32[]{:S(2)}) copy-start(bf16[64,4000]{1,0:T(8,128)(2,1)} %param.8) | copy-start | bytes 1536004
  10.6 107.1 %all-to-all-start.3 = ((bf16[32,64,928]{2,1,0:T(8,128)(2,1)}), bf16[32,64,928]{2,1,0:T(8,128)(2,1)}, u32[]{:S(2)}, u32[]{:S(2)}) async-start(bf16[32,64,928]{2,1,0:T(8,128)(2,1)} %stack.41), calls=%async_computation.3 | async-start | bytes 8388608 | tf_op jit(solution)/shard_map/all_to_all | solution.py:53
  223.1 100.3 %all-to-all-start = ((bf16[32,64,1024]{2,1,0:T(8,128)(2,1)}), bf16[32,64,1024]{2,1,0:T(8,128)(2,1)}, u32[]{:S(2)}, u32[]{:S(2)}) async-start(bf16[32,64,1024]{2,1,0:T(8,128)(2,1)} %stack.38), calls=%async_computation | async-start | bytes 8388608 | tf_op jit(solution)/shard_map/all_to_all | solution.py:53
  228.3 105.0 %all-gather.2.cloned.1.call-start = ((), (), s32[]{:S(2)}) async-start(), calls=%async_computation.4 | async-start | bytes 3538944 | tf_op jit(solution)/shard_map/all_gather | solution.py:41
  325.8 6.7 %copy-start.4 = (bf16[2048]{0:T(1024)(128)(2,1)S(1)}, bf16[2048]{0:T(1024)(128)(2,1)}, u32[]{:S(2)}) copy-start(bf16[2048]{0:T(1024)(128)(2,1)} %param.7) | copy-start | bytes 12292
  325.8 6.7 %copy-start.6 = (s32[64]{0:T(128)S(1)}, s32[64]{0:T(128)}, u32[]{:S(2)}) copy-start(s32[64]{0:T(128)} %param.10) | copy-start | bytes 772
  325.8 6.7 %copy-start.7 = (s32[64]{0:T(128)S(1)}, s32[64]{0:T(128)}, u32[]{:S(2)}) copy-start(s32[64]{0:T(128)} %param.11) | copy-start | bytes 772
  325.8 7.4 %copy-start.5 = (s32[768]{0:T(1024)S(1)}, s32[768]{0:T(1024)}, u32[]{:S(2)}) copy-start(s32[768]{0:T(1024)} %param.9) | copy-start | bytes 9220
  325.8 100.9 %all-to-all-start.2 = ((bf16[32,64,1024]{2,1,0:T(8,128)(2,1)}), bf16[32,64,1024]{2,1,0:T(8,128)(2,1)}, u32[]{:S(2)}, u32[]{:S(2)}) async-start(bf16[32,64,1024]{2,1,0:T(8,128)(2,1)} %stack.40), calls=%async_computation.2 | async-start | bytes 8388608 | tf_op jit(solution)/shard_map/all_to_all | solution.py:53
  333.3 2.8 copy-start.2
  342.9 5.7 %copy-start = (bf16[32,64,1024]{2,1,0:T(8,128)(2,1)S(1)}, bf16[32,64,1024]{2,1,0:T(8,128)(2,1)}, u32[]{:S(2)}) copy-start(bf16[32,64,1024]{2,1,0:T(8,128)(2,1)} %all_to_all.20) | copy-start | bytes 12582916
  426.8 6.6 %copy-start.1 = (f32[768,1024]{1,0:T(8,128)S(1)}, f32[768,1024]{1,0:T(8,128)}, u32[]{:S(2)}) copy-start(f32[768,1024]{1,0:T(8,128)} %get-tuple-element.35) | copy-start | bytes 9437188
Sparse Core Ops, SparseCore 0:
  231.0 35.1 all-gather.1
